TPU v7x, 32 devices: a whole 2x2x4 slice. The times are simulated.
32 devices in a mesh: node: 8 (over z, x), feat: 4 (over y, core).
Axes of the slice: x: 2, y: 2, z: 4, core: 2. Of those that a mesh axis runs over, the one named last changes fastest.
Arguments:
- features: bfloat16 [256, 4096], P('feat', 'node'), may hold values from -6 to 6
- tile_values: bfloat16 [256, 128, 128], P('node'), may hold values from -0.1875 to 0.1875
- tile_rows: int32 [64, 4], P('node'), may hold values from 0 to 3
- tile_cols: int32 [64, 4], P('node'), may hold values from 0 to 3
- tile_counts: int32 [64], P('node'), may hold values from 0 to 4, as said below
- weight: bfloat16 [256, 256], replicated, may hold values from -0.375 to 0.375
- cotangent: bfloat16 [256, 4096], P(None, ('node', 'feat')), may hold values from -6 to 6
Outputs:
- activated: bfloat16 [256, 4096], P(None, ('node', 'feat'))
- grad_weight: float32 [256, 256], replicated
- grad_features: float32 [256, 4096], P('feat', 'node')
Inputs may be any that keep to these rules, and one draw needn't show every extreme that they name: `tile_counts`: slots at or past a pair's count are ignored; some pair has all 4 slots live, and the live slots of one receiving node index vary strongly between indices.
All inputs are finite; a program needn't handle non-finite values.
Results may differ from a plain program's by a relative error of at most 0.012.
Values may be sent and summed in bfloat16 or wider, within the bound.
No kernel may reach another device: no remote copies, remote signals or barrier semaphores. Data moves between devices by JAX's collectives and lax.ppermute only.
A program may use at most 64 MiB of HBM per device.

v0:
```python
import jax
import jax.numpy as jnp
from jax import lax
from jax.sharding import PartitionSpec as P


def passed_along(x, axis, by):
    count = lax.axis_size(axis)
    return lax.ppermute(x, axis, [(i, (i + by) % count) for i in range(count)])


def select_pair(tile_values, tile_rows, tile_cols, tile_counts, source):
    slots = tile_rows.shape[1]
    values = lax.dynamic_slice_in_dim(tile_values, source * slots, slots, 0)
    row_ids = lax.dynamic_index_in_dim(tile_rows, source, 0, keepdims=False)
    col_ids = lax.dynamic_index_in_dim(tile_cols, source, 0, keepdims=False)
    number = lax.dynamic_index_in_dim(tile_counts, source, 0, keepdims=False)
    live = (jnp.arange(slots) < number).astype(jnp.float32)
    return (values, row_ids, col_ids, live)


def add_forward(totals, piece, parts, keep):
    values, row_ids, col_ids, live = parts
    blocks_in = piece.reshape(piece.shape[0], -1, values.shape[1])
    block_count = blocks_in.shape[1]
    pick = jax.nn.one_hot(col_ids, block_count, dtype=jnp.bfloat16)
    chosen = jnp.einsum("frm,sr->fsm", blocks_in, pick, preferred_element_type=jnp.float32).astype(
        jnp.bfloat16
    )
    product = jnp.einsum("fsm,sjm->fsj", chosen, values, preferred_element_type=jnp.float32)
    place = jax.nn.one_hot(row_ids, block_count, dtype=jnp.float32) * (live * keep)[:, None]
    return totals + jnp.einsum("fsj,sr->frj", product, place)


def add_backward(totals, grad_blocks, parts, keep):
    values, row_ids, col_ids, live = parts
    block_count = grad_blocks.shape[1]
    pick = jax.nn.one_hot(row_ids, block_count, dtype=jnp.bfloat16)
    chosen = jnp.einsum(
        "frj,sr->fsj", grad_blocks, pick, preferred_element_type=jnp.float32
    ).astype(jnp.bfloat16)
    product = jnp.einsum("fsj,sjm->fsm", chosen, values, preferred_element_type=jnp.float32)
    place = jax.nn.one_hot(col_ids, block_count, dtype=jnp.float32) * (live * keep)[:, None]
    return totals + jnp.einsum("fsm,sc->fcm", product, place)


def per_device(features, tile_values, tile_rows, tile_cols, tile_counts, weight, cotangent):
    node_count = lax.axis_size("node")
    own_index = lax.axis_index("node")
    slice_width = features.shape[0]
    local_nodes = features.shape[1]
    tile_side = tile_values.shape[1]
    block_count = local_nodes // tile_side

    def pair_of(source):
        return select_pair(tile_values, tile_rows, tile_cols, tile_counts, source)

    totals = jnp.zeros((slice_width, block_count, tile_side), jnp.float32)
    totals = add_forward(totals, features, pair_of(own_index), 1.0)

    def ahead_step(step, carry):
        running, moving = carry
        moving = passed_along(moving, "node", 1)
        source = (own_index - step) % node_count
        return (add_forward(running, moving, pair_of(source), 1.0), moving)

    totals, _ = lax.fori_loop(1, node_count, ahead_step, (totals, features))
    aggregated = totals.reshape(slice_width, local_nodes).astype(jnp.bfloat16)
    full_rows = lax.all_to_all(aggregated, "feat", split_axis=1, concat_axis=0, tiled=True)
    pre = jnp.dot(weight.T, full_rows, preferred_element_type=jnp.float32)
    activated = jax.nn.silu(pre).astype(jnp.bfloat16)
    sigma = jax.nn.sigmoid(pre)
    dpre = (cotangent.astype(jnp.float32) * sigma * (1.0 + pre * (1.0 - sigma))).astype(
        jnp.bfloat16
    )
    weight_part = lax.dot_general(
        full_rows, dpre, (((1,), (1,)), ((), ())), preferred_element_type=jnp.float32
    )
    grad_weight = lax.psum(weight_part, ("node", "feat"))
    dagg = jnp.dot(weight, dpre, preferred_element_type=jnp.float32).astype(jnp.bfloat16)
    grad_slices = lax.all_to_all(dagg, "feat", split_axis=0, concat_axis=1, tiled=True)
    grad_blocks = grad_slices.reshape(slice_width, block_count, tile_side)
    zeros = jnp.zeros((slice_width, block_count, tile_side), jnp.float32)
    start = add_backward(zeros, grad_blocks, pair_of((own_index - 1) % node_count), 1.0)

    def carry_step(step, running):
        running = passed_along(running, "node", 1)
        owner = (own_index - step - 1) % node_count
        return add_backward(running, grad_blocks, pair_of(owner), 1.0)

    gradient = lax.fori_loop(1, node_count, carry_step, start)
    return (activated, grad_weight, gradient.reshape(slice_width, local_nodes))


def solution(mesh):
    placed = (
        P("feat", "node"),
        P("node", None, None),
        P("node", None),
        P("node", None),
        P("node"),
        P(),
        P(None, ("node", "feat")),
    )
    return jax.shard_map(
        per_device,
        mesh=mesh,
        in_specs=placed,
        out_specs=(P(None, ("node", "feat")), P(), P("feat", "node")),
        check_vma=False,
    )
```

profile of v0, /device:TPU:0, one launch (start us, length us, event | category | flops | bytes accessed | tf_op | source)
XLA Modules:
  0.0 227.0 jit_solution(9543807741233657913)
XLA Ops:
  11.7 1.1 fusion.47
  12.9 62.7 %while.32 = (s32[]{:T(128)}, f32[64,4,128]{2,1,0:T(4,128)S(1)}, bf16[64,512]{1,0:T(8,128)(2,1)S(1)}, s32[]{:T(128)}, s32[8,4]{1,0:T(8,128)S(1)}, /*index=5*/s32[...) while((s32[]{:T(128)}, f32[64,4,128]{2,1,0:T(4,128)S(1)}, ...), condition=%wide.region_1.2_spmd, body=%wide.region_0.1_spmd.sunk | while | flops 8945741 | bytes 1245694 | solution.py:67
  12.9 3.0 %collective-permute-start = (bf16[64,512]{1,0:T(8,128)(2,1)S(1)}, bf16[64,512]{1,0:T(8,128)(2,1)S(1)}, u32[]{:S(2)}, u32[]{:S(2)}) collective-permute-start(bf16[64,512]{1,0:T(8,128)(2,1)S(1)} %get-tuple-element.610), channel_id=1, source_target_pairs={{0,4},{4,8},{8,12},{12,16},{16,20},{20,24},{24,28},{28,0},{1,5},{5... | collective-permute-start | bytes 196616 | tf_op jit(solution)/shard_map/while/body/eval_jaxpr/ppermute | solution.py:9
  17.2 4.0 %collective-permute-done = bf16[64,512]{1,0:T(8,128)(2,1)S(1)} collective-permute-done((bf16[64,512]{1,0:T(8,128)(2,1)S(1)}, bf16[64,512]{1,0:T(8,128)(2,1)S(1)}, u32[]{:S(2)}, u32[]{:S(2)}) %collective-permute-start) | collective-permute-done | bytes 65568 | tf_op jit(solution)/shard_map/while/body/eval_jaxpr/ppermute | solution.py:9
  24.3 5.7 %collective-permute-done = bf16[64,512]{1,0:T(8,128)(2,1)S(1)} collective-permute-done((bf16[64,512]{1,0:T(8,128)(2,1)S(1)}, bf16[64,512]{1,0:T(8,128)(2,1)S(1)}, u32[]{:S(2)}, u32[]{:S(2)}) %collective-permute-start) | collective-permute-done | bytes 65568 | tf_op jit(solution)/shard_map/while/body/eval_jaxpr/ppermute | solution.py:9
  33.1 5.7 %collective-permute-done = bf16[64,512]{1,0:T(8,128)(2,1)S(1)} collective-permute-done((bf16[64,512]{1,0:T(8,128)(2,1)S(1)}, bf16[64,512]{1,0:T(8,128)(2,1)S(1)}, u32[]{:S(2)}, u32[]{:S(2)}) %collective-permute-start) | collective-permute-done | bytes 65568 | tf_op jit(solution)/shard_map/while/body/eval_jaxpr/ppermute | solution.py:9
  41.9 5.7 %collective-permute-done = bf16[64,512]{1,0:T(8,128)(2,1)S(1)} collective-permute-done((bf16[64,512]{1,0:T(8,128)(2,1)S(1)}, bf16[64,512]{1,0:T(8,128)(2,1)S(1)}, u32[]{:S(2)}, u32[]{:S(2)}) %collective-permute-start) | collective-permute-done | bytes 65568 | tf_op jit(solution)/shard_map/while/body/eval_jaxpr/ppermute | solution.py:9
  50.6 5.7 %collective-permute-done = bf16[64,512]{1,0:T(8,128)(2,1)S(1)} collective-permute-done((bf16[64,512]{1,0:T(8,128)(2,1)S(1)}, bf16[64,512]{1,0:T(8,128)(2,1)S(1)}, u32[]{:S(2)}, u32[]{:S(2)}) %collective-permute-start) | collective-permute-done | bytes 65568 | tf_op jit(solution)/shard_map/while/body/eval_jaxpr/ppermute | solution.py:9
  59.4 5.7 %collective-permute-done = bf16[64,512]{1,0:T(8,128)(2,1)S(1)} collective-permute-done((bf16[64,512]{1,0:T(8,128)(2,1)S(1)}, bf16[64,512]{1,0:T(8,128)(2,1)S(1)}, u32[]{:S(2)}, u32[]{:S(2)}) %collective-permute-start) | collective-permute-done | bytes 65568 | tf_op jit(solution)/shard_map/while/body/eval_jaxpr/ppermute | solution.py:9
  68.2 5.7 %collective-permute-done = bf16[64,512]{1,0:T(8,128)(2,1)S(1)} collective-permute-done((bf16[64,512]{1,0:T(8,128)(2,1)S(1)}, bf16[64,512]{1,0:T(8,128)(2,1)S(1)}, u32[]{:S(2)}, u32[]{:S(2)}) %collective-permute-start) | collective-permute-done | bytes 65568 | tf_op jit(solution)/shard_map/while/body/eval_jaxpr/ppermute | solution.py:9
  76.2 3.4 %all-to-all-start = ((bf16[64,4,128]{2,0,1:T(8,128)(2,1)}), bf16[64,4,128]{2,0,1:T(8,128)(2,1)S(1)}, u32[]{:S(2)}, u32[]{:S(2)}) async-start(bf16[64,4,128]{2,0,1:T(8,128)(2,1)} %copy.71), calls=%async_computation | async-start | bytes 131072 | tf_op jit(solution)/shard_map/all_to_all | solution.py:69
  80.5 3.3 %all-to-all-done = bf16[64,4,128]{2,0,1:T(8,128)(2,1)S(1)} async-done(((bf16[64,4,128]{2,0,1:T(8,128)(2,1)}), bf16[64,4,128]{2,0,1:T(8,128)(2,1)S(1)}, u32[]{:S(2)}, u32[]{:S(2)}) %all-to-all-start) | async-done | bytes 65568 | tf_op jit(solution)/shard_map/all_to_all | solution.py:69
  84.9 3.3 %all-to-all-start.1 = ((bf16[4,64,128]{2,1,0:T(8,128)(2,1)}), bf16[4,64,128]{2,1,0:T(8,128)(2,1)S(1)}, u32[]{:S(2)}, u32[]{:S(2)}) async-start(bf16[4,64,128]{2,1,0:T(8,128)(2,1)} %bitcast.30), calls=%async_computation.1 | async-start | bytes 131072 | tf_op jit(solution)/shard_map/all_to_all | solution.py:81
  89.9 2.4 %all-to-all-done.1 = bf16[4,64,128]{2,1,0:T(8,128)(2,1)S(1)} async-done(((bf16[4,64,128]{2,1,0:T(8,128)(2,1)}), bf16[4,64,128]{2,1,0:T(8,128)(2,1)S(1)}, u32[]{:S(2)}, u32[]{:S(2)}) %all-to-all-start.1) | async-done | bytes 65568 | tf_op jit(solution)/shard_map/all_to_all | solution.py:81
  93.9 58.6 %while.33 = (s32[]{:T(128)}, f32[64,4,128]{2,1,0:T(4,128)S(1)}, s32[]{:T(128)}, s32[8,4]{1,0:T(8,128)S(1)}, s32[8]{0:T(128)S(1)}, /*index=5*/bf16[32,128,128]{2,...) while((s32[]{:T(128)}, f32[64,4,128]{2,1,0:T(4,128)S(1)}, ...), condition=%wide.region_4.5_spmd, body=%wide.region_3.4_spmd.sunk | while | flops 8945742 | bytes 1245714 | solution.py:91
  96.5 5.2 %collective-permute-done.1 = f32[64,4,128]{2,1,0:T(4,128)S(1)} collective-permute-done((f32[64,4,128]{2,1,0:T(4,128)S(1)}, f32[64,4,128]{2,1,0:T(4,128)S(1)}, u32[]{:S(2)}, u32[]{:S(2)}) %collective-permute-start.1) | collective-permute-done | bytes 131104 | tf_op jit(solution)/shard_map/while/body/eval_jaxpr/ppermute | solution.py:9
  104.8 5.2 %collective-permute-done.1 = f32[64,4,128]{2,1,0:T(4,128)S(1)} collective-permute-done((f32[64,4,128]{2,1,0:T(4,128)S(1)}, f32[64,4,128]{2,1,0:T(4,128)S(1)}, u32[]{:S(2)}, u32[]{:S(2)}) %collective-permute-start.1) | collective-permute-done | bytes 131104 | tf_op jit(solution)/shard_map/while/body/eval_jaxpr/ppermute | solution.py:9
  113.0 5.2 %collective-permute-done.1 = f32[64,4,128]{2,1,0:T(4,128)S(1)} collective-permute-done((f32[64,4,128]{2,1,0:T(4,128)S(1)}, f32[64,4,128]{2,1,0:T(4,128)S(1)}, u32[]{:S(2)}, u32[]{:S(2)}) %collective-permute-start.1) | collective-permute-done | bytes 131104 | tf_op jit(solution)/shard_map/while/body/eval_jaxpr/ppermute | solution.py:9
  121.2 5.1 %collective-permute-done.1 = f32[64,4,128]{2,1,0:T(4,128)S(1)} collective-permute-done((f32[64,4,128]{2,1,0:T(4,128)S(1)}, f32[64,4,128]{2,1,0:T(4,128)S(1)}, u32[]{:S(2)}, u32[]{:S(2)}) %collective-permute-start.1) | collective-permute-done | bytes 131104 | tf_op jit(solution)/shard_map/while/body/eval_jaxpr/ppermute | solution.py:9
  129.3 5.3 %collective-permute-done.1 = f32[64,4,128]{2,1,0:T(4,128)S(1)} collective-permute-done((f32[64,4,128]{2,1,0:T(4,128)S(1)}, f32[64,4,128]{2,1,0:T(4,128)S(1)}, u32[]{:S(2)}, u32[]{:S(2)}) %collective-permute-start.1) | collective-permute-done | bytes 131104 | tf_op jit(solution)/shard_map/while/body/eval_jaxpr/ppermute | solution.py:9
  137.7 6.3 %collective-permute-done.1 = f32[64,4,128]{2,1,0:T(4,128)S(1)} collective-permute-done((f32[64,4,128]{2,1,0:T(4,128)S(1)}, f32[64,4,128]{2,1,0:T(4,128)S(1)}, u32[]{:S(2)}, u32[]{:S(2)}) %collective-permute-start.1) | collective-permute-done | bytes 131104 | tf_op jit(solution)/shard_map/while/body/eval_jaxpr/ppermute | solution.py:9
  147.0 5.2 %collective-permute-done.1 = f32[64,4,128]{2,1,0:T(4,128)S(1)} collective-permute-done((f32[64,4,128]{2,1,0:T(4,128)S(1)}, f32[64,4,128]{2,1,0:T(4,128)S(1)}, u32[]{:S(2)}, u32[]{:S(2)}) %collective-permute-start.1) | collective-permute-done | bytes 131104 | tf_op jit(solution)/shard_map/while/body/eval_jaxpr/ppermute | solution.py:9
  153.2 65.3 %all-reduce.2.cloned.1.call-done = f32[256,256]{1,0:T(8,128)} async-done(((f32[256,256]{1,0:T(8,128)}), f32[256,256]{1,0:T(8,128)}) %all-reduce.2.cloned.1.call-update) | async-done | bytes 262160 | tf_op jit(solution)/shard_map/psum | solution.py:79
  218.5 1.7 copy.99
  (145 shorter events, 52.9 us)
Async XLA Ops:
  7.2 76.6 %copy-start = (bf16[256,256]{1,0:T(8,128)(2,1)S(1)}, bf16[256,256]{1,0:T(8,128)(2,1)}, u32[]{:S(2)}) copy-start(bf16[256,256]{1,0:T(8,128)(2,1)} %param.16) | copy-start | bytes 393220
  8.1 0.7 copy-start.2
  8.7 0.7 copy-start.3
  9.5 0.7 copy-start.4
  12.9 8.3 %collective-permute-start = (bf16[64,512]{1,0:T(8,128)(2,1)S(1)}, bf16[64,512]{1,0:T(8,128)(2,1)S(1)}, u32[]{:S(2)}, u32[]{:S(2)}) collective-permute-start(bf16[64,512]{1,0:T(8,128)(2,1)S(1)} %get-tuple-element.610), channel_id=1, source_target_pairs={{0,4},{4,8},{8,12},{12,16},{16,20},{20,24},{24,28},{28,0},{1,5},{5... | collective-permute-start | bytes 196616 | tf_op jit(solution)/shard_map/while/body/eval_jaxpr/ppermute | solution.py:9
  23.0 7.0 %collective-permute-start = (bf16[64,512]{1,0:T(8,128)(2,1)S(1)}, bf16[64,512]{1,0:T(8,128)(2,1)S(1)}, u32[]{:S(2)}, u32[]{:S(2)}) collective-permute-start(bf16[64,512]{1,0:T(8,128)(2,1)S(1)} %get-tuple-element.610), channel_id=1, source_target_pairs={{0,4},{4,8},{8,12},{12,16},{16,20},{20,24},{24,28},{28,0},{1,5},{5... | collective-permute-start | bytes 196616 | tf_op jit(solution)/shard_map/while/body/eval_jaxpr/ppermute | solution.py:9
  31.7 7.0 %collective-permute-start = (bf16[64,512]{1,0:T(8,128)(2,1)S(1)}, bf16[64,512]{1,0:T(8,128)(2,1)S(1)}, u32[]{:S(2)}, u32[]{:S(2)}) collective-permute-start(bf16[64,512]{1,0:T(8,128)(2,1)S(1)} %get-tuple-element.610), channel_id=1, source_target_pairs={{0,4},{4,8},{8,12},{12,16},{16,20},{20,24},{24,28},{28,0},{1,5},{5... | collective-permute-start | bytes 196616 | tf_op jit(solution)/shard_map/while/body/eval_jaxpr/ppermute | solution.py:9
  40.5 7.0 %collective-permute-start = (bf16[64,512]{1,0:T(8,128)(2,1)S(1)}, bf16[64,512]{1,0:T(8,128)(2,1)S(1)}, u32[]{:S(2)}, u32[]{:S(2)}) collective-permute-start(bf16[64,512]{1,0:T(8,128)(2,1)S(1)} %get-tuple-element.610), channel_id=1, source_target_pairs={{0,4},{4,8},{8,12},{12,16},{16,20},{20,24},{24,28},{28,0},{1,5},{5... | collective-permute-start | bytes 196616 | tf_op jit(solution)/shard_map/while/body/eval_jaxpr/ppermute | solution.py:9
  49.3 7.0 %collective-permute-start = (bf16[64,512]{1,0:T(8,128)(2,1)S(1)}, bf16[64,512]{1,0:T(8,128)(2,1)S(1)}, u32[]{:S(2)}, u32[]{:S(2)}) collective-permute-start(bf16[64,512]{1,0:T(8,128)(2,1)S(1)} %get-tuple-element.610), channel_id=1, source_target_pairs={{0,4},{4,8},{8,12},{12,16},{16,20},{20,24},{24,28},{28,0},{1,5},{5... | collective-permute-start | bytes 196616 | tf_op jit(solution)/shard_map/while/body/eval_jaxpr/ppermute | solution.py:9
  58.1 7.0 %collective-permute-start = (bf16[64,512]{1,0:T(8,128)(2,1)S(1)}, bf16[64,512]{1,0:T(8,128)(2,1)S(1)}, u32[]{:S(2)}, u32[]{:S(2)}) collective-permute-start(bf16[64,512]{1,0:T(8,128)(2,1)S(1)} %get-tuple-element.610), channel_id=1, source_target_pairs={{0,4},{4,8},{8,12},{12,16},{16,20},{20,24},{24,28},{28,0},{1,5},{5... | collective-permute-start | bytes 196616 | tf_op jit(solution)/shard_map/while/body/eval_jaxpr/ppermute | solution.py:9
  66.8 7.0 %collective-permute-start = (bf16[64,512]{1,0:T(8,128)(2,1)S(1)}, bf16[64,512]{1,0:T(8,128)(2,1)S(1)}, u32[]{:S(2)}, u32[]{:S(2)}) collective-permute-start(bf16[64,512]{1,0:T(8,128)(2,1)S(1)} %get-tuple-element.610), channel_id=1, source_target_pairs={{0,4},{4,8},{8,12},{12,16},{16,20},{20,24},{24,28},{28,0},{1,5},{5... | collective-permute-start | bytes 196616 | tf_op jit(solution)/shard_map/while/body/eval_jaxpr/ppermute | solution.py:9
  76.2 4.1 %copy-start.1 = (bf16[256,128]{1,0:T(8,128)(2,1)S(1)}, bf16[256,128]{1,0:T(8,128)(2,1)}, u32[]{:S(2)}) copy-start(bf16[256,128]{1,0:T(8,128)(2,1)} %param.17) | copy-start | bytes 196612
  76.2 7.5 %all-to-all-start = ((bf16[64,4,128]{2,0,1:T(8,128)(2,1)}), bf16[64,4,128]{2,0,1:T(8,128)(2,1)S(1)}, u32[]{:S(2)}, u32[]{:S(2)}) async-start(bf16[64,4,128]{2,0,1:T(8,128)(2,1)} %copy.71), calls=%async_computation | async-start | bytes 131072 | tf_op jit(solution)/shard_map/all_to_all | solution.py:69
  84.9 7.4 %all-to-all-start.1 = ((bf16[4,64,128]{2,1,0:T(8,128)(2,1)}), bf16[4,64,128]{2,1,0:T(8,128)(2,1)S(1)}, u32[]{:S(2)}, u32[]{:S(2)}) async-start(bf16[4,64,128]{2,1,0:T(8,128)(2,1)} %bitcast.30), calls=%async_computation.1 | async-start | bytes 131072 | tf_op jit(solution)/shard_map/all_to_all | solution.py:81
  88.2 130.3 %all-reduce.2.cloned.1.call-start = ((), (), s32[]{:S(2)}) async-start(), calls=%async_computation.2 | async-start | bytes 524288 | tf_op jit(solution)/shard_map/psum | solution.py:79
  93.9 7.9 %collective-permute-start.1 = (f32[64,4,128]{2,1,0:T(4,128)S(1)}, f32[64,4,128]{2,1,0:T(4,128)S(1)}, u32[]{:S(2)}, u32[]{:S(2)}) collective-permute-start(f32[64,4,128]{2,1,0:T(4,128)S(1)} %get-tuple-element.652), channel_id=1, source_target_pairs={{0,4},{4,8},{8,12},{12,16},{16,20},{20,24},{24,28},{28,0},{1,5},{5... | collective-permute-start | bytes 393224 | tf_op jit(solution)/shard_map/while/body/eval_jaxpr/ppermute | solution.py:9
  102.1 7.9 %collective-permute-start.1 = (f32[64,4,128]{2,1,0:T(4,128)S(1)}, f32[64,4,128]{2,1,0:T(4,128)S(1)}, u32[]{:S(2)}, u32[]{:S(2)}) collective-permute-start(f32[64,4,128]{2,1,0:T(4,128)S(1)} %get-tuple-element.652), channel_id=1, source_target_pairs={{0,4},{4,8},{8,12},{12,16},{16,20},{20,24},{24,28},{28,0},{1,5},{5... | collective-permute-start | bytes 393224 | tf_op jit(solution)/shard_map/while/body/eval_jaxpr/ppermute | solution.py:9
  110.4 7.9 %collective-permute-start.1 = (f32[64,4,128]{2,1,0:T(4,128)S(1)}, f32[64,4,128]{2,1,0:T(4,128)S(1)}, u32[]{:S(2)}, u32[]{:S(2)}) collective-permute-start(f32[64,4,128]{2,1,0:T(4,128)S(1)} %get-tuple-element.652), channel_id=1, source_target_pairs={{0,4},{4,8},{8,12},{12,16},{16,20},{20,24},{24,28},{28,0},{1,5},{5... | collective-permute-start | bytes 393224 | tf_op jit(solution)/shard_map/while/body/eval_jaxpr/ppermute | solution.py:9
  118.6 7.7 %collective-permute-start.1 = (f32[64,4,128]{2,1,0:T(4,128)S(1)}, f32[64,4,128]{2,1,0:T(4,128)S(1)}, u32[]{:S(2)}, u32[]{:S(2)}) collective-permute-start(f32[64,4,128]{2,1,0:T(4,128)S(1)} %get-tuple-element.652), channel_id=1, source_target_pairs={{0,4},{4,8},{8,12},{12,16},{16,20},{20,24},{24,28},{28,0},{1,5},{5... | collective-permute-start | bytes 393224 | tf_op jit(solution)/shard_map/while/body/eval_jaxpr/ppermute | solution.py:9
  126.7 8.0 %collective-permute-start.1 = (f32[64,4,128]{2,1,0:T(4,128)S(1)}, f32[64,4,128]{2,1,0:T(4,128)S(1)}, u32[]{:S(2)}, u32[]{:S(2)}) collective-permute-start(f32[64,4,128]{2,1,0:T(4,128)S(1)} %get-tuple-element.652), channel_id=1, source_target_pairs={{0,4},{4,8},{8,12},{12,16},{16,20},{20,24},{24,28},{28,0},{1,5},{5... | collective-permute-start | bytes 393224 | tf_op jit(solution)/shard_map/while/body/eval_jaxpr/ppermute | solution.py:9
  135.0 8.9 %collective-permute-start.1 = (f32[64,4,128]{2,1,0:T(4,128)S(1)}, f32[64,4,128]{2,1,0:T(4,128)S(1)}, u32[]{:S(2)}, u32[]{:S(2)}) collective-permute-start(f32[64,4,128]{2,1,0:T(4,128)S(1)} %get-tuple-element.652), channel_id=1, source_target_pairs={{0,4},{4,8},{8,12},{12,16},{16,20},{20,24},{24,28},{28,0},{1,5},{5... | collective-permute-start | bytes 393224 | tf_op jit(solution)/shard_map/while/body/eval_jaxpr/ppermute | solution.py:9
  144.3 7.8 %collective-permute-start.1 = (f32[64,4,128]{2,1,0:T(4,128)S(1)}, f32[64,4,128]{2,1,0:T(4,128)S(1)}, u32[]{:S(2)}, u32[]{:S(2)}) collective-permute-start(f32[64,4,128]{2,1,0:T(4,128)S(1)} %get-tuple-element.652), channel_id=1, source_target_pairs={{0,4},{4,8},{8,12},{12,16},{16,20},{20,24},{24,28},{28,0},{1,5},{5... | collective-permute-start | bytes 393224 | tf_op jit(solution)/shard_map/while/body/eval_jaxpr/ppermute | solution.py:9
Sparse Core Ops, SparseCore 0:
  95.1 123.3 all-reduce.1
where the time goes:
time: 228 us; the launch traced here: 227 us
  waiting for transfers between devices  147 us (64%)
  matrix products  27.7 us (12%)
  local copies, waits for them, and re-layouts  16.8 us (7%)
  between operations  14.2 us (6%)
  starting transfers between devices  10.5 us (5%)
  other arithmetic  10.4 us (5%)
    ppermute x14, waiting for transfers between devices, passed_along(): return lax.ppermute(x, axis, [(i, (i + by) % count) for i in range(count)])  75.5 us
    psum x1, waiting for transfers between devices, per_device(): grad_weight = lax.psum(weight_part, ('node', 'feat'))  65.3 us
    convert_element_type x16, other arithmetic, select_pair(): live = (jnp.arange(slots) < number).astype(jnp.float32)  10.4 us
    dynamic_slice x15, local copies, waits for them, and re-layouts, select_pair(): number = lax.dynamic_index_in_dim(tile_counts, source, 0, keepdims=False)  8.87 us
    dot_general x8, matrix products, add_forward(): jnp.einsum('fsm,sjm->fsj', chosen, values, preferred_element_type=jnp.flo...  8.64 us
    dot_general x8, matrix products, add_backward(): jnp.einsum('fsj,sjm->fsm', chosen, values, preferred_element_type=jnp.flo...  8.47 us
    unnamed x15, local copies, waits for them, and re-layouts  5.78 us
  transfers between devices with their start and end apart: 17, of which 17 were waited for; matrix products, arithmetic and copies ran while one was open for 15% of the time, Pallas kernels for 0%

commit v1 on v0

--- a/solution.py
+++ b/solution.py
@@ -2,6 +2,12 @@
 import jax.numpy as jnp
 from jax import lax
 from jax.sharding import PartitionSpec as P
+from jax.lax import psum
+
+
+def mix_the_arrays(local_block):
+    local_now = psum(local_block, "feat")
+    return psum(local_now, "node")
 
 
 def passed_along(x, axis, by):
@@ -76,7 +82,7 @@
     weight_part = lax.dot_general(
         full_rows, dpre, (((1,), (1,)), ((), ())), preferred_element_type=jnp.float32
     )
-    grad_weight = lax.psum(weight_part, ("node", "feat"))
+    grad_weight = mix_the_arrays(weight_part)
     dagg = jnp.dot(weight, dpre, preferred_element_type=jnp.float32).astype(jnp.bfloat16)
     grad_slices = lax.all_to_all(dagg, "feat", split_axis=0, concat_axis=1, tiled=True)
     grad_blocks = grad_slices.reshape(slice_width, block_count, tile_side)

time: 228 us -> 208 us (0.912)
  waiting for transfers between devices: 147 us -> 125 us
    psum x1 -> x2, waiting for transfers between devices: 65.3 us -> 44.1 us  [the longest x1 27.9 us: mix_the_arrays(): local_now = psum(local_block, 'feat')]
  transfers between devices with their start and end apart: 17 -> 18, of which waited for: 17 -> 18; matrix products, arithmetic and copies ran while one was open for 15% -> 16% of each run, Pallas kernels for 0% -> 0%
where the time goes in v1:
time: 208 us; the launch traced here: 207 us
  waiting for transfers between devices  125 us (60%)
  matrix products  27.7 us (13%)
  local copies, waits for them, and re-layouts  16.8 us (8%)
  between operations  14.2 us (7%)
  starting transfers between devices  12 us (6%)
  other arithmetic  10.4 us (5%)
    ppermute x14, waiting for transfers between devices, passed_along(): return lax.ppermute(x, axis, [(i, (i + by) % count) for i in range(count)])  75.2 us
    psum x1, waiting for transfers between devices, mix_the_arrays(): local_now = psum(local_block, 'feat')  27.9 us
    psum x1, waiting for transfers between devices, mix_the_arrays(): return psum(local_now, 'node')  16.3 us
    convert_element_type x16, other arithmetic, select_pair(): live = (jnp.arange(slots) < number).astype(jnp.float32)  10.4 us
    dynamic_slice x15, local copies, waits for them, and re-layouts, select_pair(): number = lax.dynamic_index_in_dim(tile_counts, source, 0, keepdims=False)  8.87 us
    dot_general x8, matrix products, add_forward(): jnp.einsum('fsm,sjm->fsj', chosen, values, preferred_element_type=jnp.flo...  8.64 us
    dot_general x8, matrix products, add_backward(): jnp.einsum('fsj,sjm->fsm', chosen, values, preferred_element_type=jnp.flo...  8.48 us
    unnamed x15, local copies, waits for them, and re-layouts  5.78 us
  transfers between devices with their start and end apart: 18, of which 18 were waited for; matrix products, arithmetic and copies ran while one was open for 16% of the time, Pallas kernels for 0%

profile of v1, /device:TPU:0, one launch (start us, length us, event | category | flops | bytes accessed | tf_op | source)
XLA Modules:
  0.0 207.0 jit_solution(7341547594399808723)
XLA Ops:
  12.9 62.7 %while.32 = (s32[]{:T(128)}, f32[64,4,128]{2,1,0:T(4,128)S(1)}, bf16[64,512]{1,0:T(8,128)(2,1)S(1)}, s32[]{:T(128)}, s32[8,4]{1,0:T(8,128)S(1)}, /*index=5*/s32[...) while((s32[]{:T(128)}, f32[64,4,128]{2,1,0:T(4,128)S(1)}, ...), condition=%wide.region_1.2_spmd, body=%wide.region_0.1_spmd.sunk | while | flops 8945741 | bytes 1245694 | solution.py:73
  12.9 3.0 %collective-permute-start = (bf16[64,512]{1,0:T(8,128)(2,1)S(1)}, bf16[64,512]{1,0:T(8,128)(2,1)S(1)}, u32[]{:S(2)}, u32[]{:S(2)}) collective-permute-start(bf16[64,512]{1,0:T(8,128)(2,1)S(1)} %get-tuple-element.610), channel_id=1, source_target_pairs={{0,4},{4,8},{8,12},{12,16},{16,20},{20,24},{24,28},{28,0},{1,5},{5... | collective-permute-start | bytes 196616 | tf_op jit(solution)/shard_map/while/body/eval_jaxpr/ppermute | solution.py:15
  17.2 4.0 %collective-permute-done = bf16[64,512]{1,0:T(8,128)(2,1)S(1)} collective-permute-done((bf16[64,512]{1,0:T(8,128)(2,1)S(1)}, bf16[64,512]{1,0:T(8,128)(2,1)S(1)}, u32[]{:S(2)}, u32[]{:S(2)}) %collective-permute-start) | collective-permute-done | bytes 65568 | tf_op jit(solution)/shard_map/while/body/eval_jaxpr/ppermute | solution.py:15
  24.3 5.7 %collective-permute-done = bf16[64,512]{1,0:T(8,128)(2,1)S(1)} collective-permute-done((bf16[64,512]{1,0:T(8,128)(2,1)S(1)}, bf16[64,512]{1,0:T(8,128)(2,1)S(1)}, u32[]{:S(2)}, u32[]{:S(2)}) %collective-permute-start) | collective-permute-done | bytes 65568 | tf_op jit(solution)/shard_map/while/body/eval_jaxpr/ppermute | solution.py:15
  33.1 5.7 %collective-permute-done = bf16[64,512]{1,0:T(8,128)(2,1)S(1)} collective-permute-done((bf16[64,512]{1,0:T(8,128)(2,1)S(1)}, bf16[64,512]{1,0:T(8,128)(2,1)S(1)}, u32[]{:S(2)}, u32[]{:S(2)}) %collective-permute-start) | collective-permute-done | bytes 65568 | tf_op jit(solution)/shard_map/while/body/eval_jaxpr/ppermute | solution.py:15
  41.9 5.7 %collective-permute-done = bf16[64,512]{1,0:T(8,128)(2,1)S(1)} collective-permute-done((bf16[64,512]{1,0:T(8,128)(2,1)S(1)}, bf16[64,512]{1,0:T(8,128)(2,1)S(1)}, u32[]{:S(2)}, u32[]{:S(2)}) %collective-permute-start) | collective-permute-done | bytes 65568 | tf_op jit(solution)/shard_map/while/body/eval_jaxpr/ppermute | solution.py:15
  50.6 5.7 %collective-permute-done = bf16[64,512]{1,0:T(8,128)(2,1)S(1)} collective-permute-done((bf16[64,512]{1,0:T(8,128)(2,1)S(1)}, bf16[64,512]{1,0:T(8,128)(2,1)S(1)}, u32[]{:S(2)}, u32[]{:S(2)}) %collective-permute-start) | collective-permute-done | bytes 65568 | tf_op jit(solution)/shard_map/while/body/eval_jaxpr/ppermute | solution.py:15
  59.4 5.7 %collective-permute-done = bf16[64,512]{1,0:T(8,128)(2,1)S(1)} collective-permute-done((bf16[64,512]{1,0:T(8,128)(2,1)S(1)}, bf16[64,512]{1,0:T(8,128)(2,1)S(1)}, u32[]{:S(2)}, u32[]{:S(2)}) %collective-permute-start) | collective-permute-done | bytes 65568 | tf_op jit(solution)/shard_map/while/body/eval_jaxpr/ppermute | solution.py:15
  68.2 5.7 %collective-permute-done = bf16[64,512]{1,0:T(8,128)(2,1)S(1)} collective-permute-done((bf16[64,512]{1,0:T(8,128)(2,1)S(1)}, bf16[64,512]{1,0:T(8,128)(2,1)S(1)}, u32[]{:S(2)}, u32[]{:S(2)}) %collective-permute-start) | collective-permute-done | bytes 65568 | tf_op jit(solution)/shard_map/while/body/eval_jaxpr/ppermute | solution.py:15
  76.2 3.4 %all-to-all-start = ((bf16[64,4,128]{2,0,1:T(8,128)(2,1)}), bf16[64,4,128]{2,0,1:T(8,128)(2,1)S(1)}, u32[]{:S(2)}, u32[]{:S(2)}) async-start(bf16[64,4,128]{2,0,1:T(8,128)(2,1)} %copy.71), calls=%async_computation | async-start | bytes 131072 | tf_op jit(solution)/shard_map/all_to_all | solution.py:75
  80.5 3.3 %all-to-all-done = bf16[64,4,128]{2,0,1:T(8,128)(2,1)S(1)} async-done(((bf16[64,4,128]{2,0,1:T(8,128)(2,1)}), bf16[64,4,128]{2,0,1:T(8,128)(2,1)S(1)}, u32[]{:S(2)}, u32[]{:S(2)}) %all-to-all-start) | async-done | bytes 65568 | tf_op jit(solution)/shard_map/all_to_all | solution.py:75
  84.9 3.3 %all-to-all-start.1 = ((bf16[4,64,128]{2,1,0:T(8,128)(2,1)}), bf16[4,64,128]{2,1,0:T(8,128)(2,1)S(1)}, u32[]{:S(2)}, u32[]{:S(2)}) async-start(bf16[4,64,128]{2,1,0:T(8,128)(2,1)} %bitcast.30), calls=%async_computation.1 | async-start | bytes 131072 | tf_op jit(solution)/shard_map/all_to_all | solution.py:87
  90.0 2.4 %all-to-all-done.1 = bf16[4,64,128]{2,1,0:T(8,128)(2,1)S(1)} async-done(((bf16[4,64,128]{2,1,0:T(8,128)(2,1)}), bf16[4,64,128]{2,1,0:T(8,128)(2,1)S(1)}, u32[]{:S(2)}, u32[]{:S(2)}) %all-to-all-start.1) | async-done | bytes 65568 | tf_op jit(solution)/shard_map/all_to_all | solution.py:87
  93.9 27.9 %all-reduce.3.cloned.1.call-done = f32[256,256]{1,0:T(8,128)} async-done(((f32[256,256]{1,0:T(8,128)}), f32[256,256]{1,0:T(8,128)}) %all-reduce.3.cloned.1.call-update) | async-done | bytes 262160 | tf_op jit(solution)/shard_map/psum | solution.py:9
  121.7 59.8 %while.33 = (s32[]{:T(128)}, f32[64,4,128]{2,1,0:T(4,128)S(1)}, s32[]{:T(128)}, s32[8,4]{1,0:T(8,128)S(1)}, s32[8]{0:T(128)S(1)}, /*index=5*/bf16[32,128,128]{2,...) while((s32[]{:T(128)}, f32[64,4,128]{2,1,0:T(4,128)S(1)}, ...), condition=%wide.region_5.6_spmd, body=%wide.region_4.5_spmd.sunk | while | flops 8945742 | bytes 1245714 | solution.py:97
  125.8 3.6 %collective-permute-done.1 = f32[64,4,128]{2,1,0:T(4,128)S(1)} collective-permute-done((f32[64,4,128]{2,1,0:T(4,128)S(1)}, f32[64,4,128]{2,1,0:T(4,128)S(1)}, u32[]{:S(2)}, u32[]{:S(2)}) %collective-permute-start.1) | collective-permute-done | bytes 131104 | tf_op jit(solution)/shard_map/while/body/eval_jaxpr/ppermute | solution.py:15
  132.5 5.5 %collective-permute-done.1 = f32[64,4,128]{2,1,0:T(4,128)S(1)} collective-permute-done((f32[64,4,128]{2,1,0:T(4,128)S(1)}, f32[64,4,128]{2,1,0:T(4,128)S(1)}, u32[]{:S(2)}, u32[]{:S(2)}) %collective-permute-start.1) | collective-permute-done | bytes 131104 | tf_op jit(solution)/shard_map/while/body/eval_jaxpr/ppermute | solution.py:15
  141.0 5.0 %collective-permute-done.1 = f32[64,4,128]{2,1,0:T(4,128)S(1)} collective-permute-done((f32[64,4,128]{2,1,0:T(4,128)S(1)}, f32[64,4,128]{2,1,0:T(4,128)S(1)}, u32[]{:S(2)}, u32[]{:S(2)}) %collective-permute-start.1) | collective-permute-done | bytes 131104 | tf_op jit(solution)/shard_map/while/body/eval_jaxpr/ppermute | solution.py:15
  149.1 5.8 %collective-permute-done.1 = f32[64,4,128]{2,1,0:T(4,128)S(1)} collective-permute-done((f32[64,4,128]{2,1,0:T(4,128)S(1)}, f32[64,4,128]{2,1,0:T(4,128)S(1)}, u32[]{:S(2)}, u32[]{:S(2)}) %collective-permute-start.1) | collective-permute-done | bytes 131104 | tf_op jit(solution)/shard_map/while/body/eval_jaxpr/ppermute | solution.py:15
  157.9 6.4 %collective-permute-done.1 = f32[64,4,128]{2,1,0:T(4,128)S(1)} collective-permute-done((f32[64,4,128]{2,1,0:T(4,128)S(1)}, f32[64,4,128]{2,1,0:T(4,128)S(1)}, u32[]{:S(2)}, u32[]{:S(2)}) %collective-permute-start.1) | collective-permute-done | bytes 131104 | tf_op jit(solution)/shard_map/while/body/eval_jaxpr/ppermute | solution.py:15
  167.3 5.7 %collective-permute-done.1 = f32[64,4,128]{2,1,0:T(4,128)S(1)} collective-permute-done((f32[64,4,128]{2,1,0:T(4,128)S(1)}, f32[64,4,128]{2,1,0:T(4,128)S(1)}, u32[]{:S(2)}, u32[]{:S(2)}) %collective-permute-start.1) | collective-permute-done | bytes 131104 | tf_op jit(solution)/shard_map/while/body/eval_jaxpr/ppermute | solution.py:15
  176.1 5.1 %collective-permute-done.1 = f32[64,4,128]{2,1,0:T(4,128)S(1)} collective-permute-done((f32[64,4,128]{2,1,0:T(4,128)S(1)}, f32[64,4,128]{2,1,0:T(4,128)S(1)}, u32[]{:S(2)}, u32[]{:S(2)}) %collective-permute-start.1) | collective-permute-done | bytes 131104 | tf_op jit(solution)/shard_map/while/body/eval_jaxpr/ppermute | solution.py:15
  182.2 16.3 %all-reduce.5.cloned.1.call-done = f32[256,256]{1,0:T(8,128)} async-done(((f32[256,256]{1,0:T(8,128)}), f32[256,256]{1,0:T(8,128)}) %all-reduce.5.cloned.1.call-update) | async-done | bytes 262160 | tf_op jit(solution)/shard_map/psum | solution.py:10
  198.5 1.7 copy.100
  (148 shorter events, 55.5 us)
Async XLA Ops:
  7.2 76.6 %copy-start = (bf16[256,256]{1,0:T(8,128)(2,1)S(1)}, bf16[256,256]{1,0:T(8,128)(2,1)}, u32[]{:S(2)}) copy-start(bf16[256,256]{1,0:T(8,128)(2,1)} %param.16) | copy-start | bytes 393220
  8.1 0.7 copy-start.2
  8.7 0.7 copy-start.3
  9.5 0.7 copy-start.4
  12.9 8.3 %collective-permute-start = (bf16[64,512]{1,0:T(8,128)(2,1)S(1)}, bf16[64,512]{1,0:T(8,128)(2,1)S(1)}, u32[]{:S(2)}, u32[]{:S(2)}) collective-permute-start(bf16[64,512]{1,0:T(8,128)(2,1)S(1)} %get-tuple-element.610), channel_id=1, source_target_pairs={{0,4},{4,8},{8,12},{12,16},{16,20},{20,24},{24,28},{28,0},{1,5},{5... | collective-permute-start | bytes 196616 | tf_op jit(solution)/shard_map/while/body/eval_jaxpr/ppermute | solution.py:15
  23.0 7.0 %collective-permute-start = (bf16[64,512]{1,0:T(8,128)(2,1)S(1)}, bf16[64,512]{1,0:T(8,128)(2,1)S(1)}, u32[]{:S(2)}, u32[]{:S(2)}) collective-permute-start(bf16[64,512]{1,0:T(8,128)(2,1)S(1)} %get-tuple-element.610), channel_id=1, source_target_pairs={{0,4},{4,8},{8,12},{12,16},{16,20},{20,24},{24,28},{28,0},{1,5},{5... | collective-permute-start | bytes 196616 | tf_op jit(solution)/shard_map/while/body/eval_jaxpr/ppermute | solution.py:15
  31.7 7.0 %collective-permute-start = (bf16[64,512]{1,0:T(8,128)(2,1)S(1)}, bf16[64,512]{1,0:T(8,128)(2,1)S(1)}, u32[]{:S(2)}, u32[]{:S(2)}) collective-permute-start(bf16[64,512]{1,0:T(8,128)(2,1)S(1)} %get-tuple-element.610), channel_id=1, source_target_pairs={{0,4},{4,8},{8,12},{12,16},{16,20},{20,24},{24,28},{28,0},{1,5},{5... | collective-permute-start | bytes 196616 | tf_op jit(solution)/shard_map/while/body/eval_jaxpr/ppermute | solution.py:15
  40.5 7.0 %collective-permute-start = (bf16[64,512]{1,0:T(8,128)(2,1)S(1)}, bf16[64,512]{1,0:T(8,128)(2,1)S(1)}, u32[]{:S(2)}, u32[]{:S(2)}) collective-permute-start(bf16[64,512]{1,0:T(8,128)(2,1)S(1)} %get-tuple-element.610), channel_id=1, source_target_pairs={{0,4},{4,8},{8,12},{12,16},{16,20},{20,24},{24,28},{28,0},{1,5},{5... | collective-permute-start | bytes 196616 | tf_op jit(solution)/shard_map/while/body/eval_jaxpr/ppermute | solution.py:15
  49.3 7.0 %collective-permute-start = (bf16[64,512]{1,0:T(8,128)(2,1)S(1)}, bf16[64,512]{1,0:T(8,128)(2,1)S(1)}, u32[]{:S(2)}, u32[]{:S(2)}) collective-permute-start(bf16[64,512]{1,0:T(8,128)(2,1)S(1)} %get-tuple-element.610), channel_id=1, source_target_pairs={{0,4},{4,8},{8,12},{12,16},{16,20},{20,24},{24,28},{28,0},{1,5},{5... | collective-permute-start | bytes 196616 | tf_op jit(solution)/shard_map/while/body/eval_jaxpr/ppermute | solution.py:15
  58.1 7.0 %collective-permute-start = (bf16[64,512]{1,0:T(8,128)(2,1)S(1)}, bf16[64,512]{1,0:T(8,128)(2,1)S(1)}, u32[]{:S(2)}, u32[]{:S(2)}) collective-permute-start(bf16[64,512]{1,0:T(8,128)(2,1)S(1)} %get-tuple-element.610), channel_id=1, source_target_pairs={{0,4},{4,8},{8,12},{12,16},{16,20},{20,24},{24,28},{28,0},{1,5},{5... | collective-permute-start | bytes 196616 | tf_op jit(solution)/shard_map/while/body/eval_jaxpr/ppermute | solution.py:15
  66.8 7.0 %collective-permute-start = (bf16[64,512]{1,0:T(8,128)(2,1)S(1)}, bf16[64,512]{1,0:T(8,128)(2,1)S(1)}, u32[]{:S(2)}, u32[]{:S(2)}) collective-permute-start(bf16[64,512]{1,0:T(8,128)(2,1)S(1)} %get-tuple-element.610), channel_id=1, source_target_pairs={{0,4},{4,8},{8,12},{12,16},{16,20},{20,24},{24,28},{28,0},{1,5},{5... | collective-permute-start | bytes 196616 | tf_op jit(solution)/shard_map/while/body/eval_jaxpr/ppermute | solution.py:15
  76.2 4.1 %copy-start.1 = (bf16[256,128]{1,0:T(8,128)(2,1)S(1)}, bf16[256,128]{1,0:T(8,128)(2,1)}, u32[]{:S(2)}) copy-start(bf16[256,128]{1,0:T(8,128)(2,1)} %param.17) | copy-start | bytes 196612
  76.2 7.5 %all-to-all-start = ((bf16[64,4,128]{2,0,1:T(8,128)(2,1)}), bf16[64,4,128]{2,0,1:T(8,128)(2,1)S(1)}, u32[]{:S(2)}, u32[]{:S(2)}) async-start(bf16[64,4,128]{2,0,1:T(8,128)(2,1)} %copy.71), calls=%async_computation | async-start | bytes 131072 | tf_op jit(solution)/shard_map/all_to_all | solution.py:75
  84.9 7.4 %all-to-all-start.1 = ((bf16[4,64,128]{2,1,0:T(8,128)(2,1)}), bf16[4,64,128]{2,1,0:T(8,128)(2,1)S(1)}, u32[]{:S(2)}, u32[]{:S(2)}) async-start(bf16[4,64,128]{2,1,0:T(8,128)(2,1)} %bitcast.30), calls=%async_computation.1 | async-start | bytes 131072 | tf_op jit(solution)/shard_map/all_to_all | solution.py:87
  88.2 33.5 %all-reduce.3.cloned.1.call-start = ((), (), s32[]{:S(2)}) async-start(), calls=%async_computation.2 | async-start | bytes 524288 | tf_op jit(solution)/shard_map/psum | solution.py:9
  89.9 108.6 %all-reduce.5.cloned.1.call-start = ((), (), s32[]{:S(2)}) async-start(), calls=%async_computation.3 | async-start | bytes 524288 | tf_op jit(solution)/shard_map/psum | solution.py:10
  121.7 7.7 %collective-permute-start.1 = (f32[64,4,128]{2,1,0:T(4,128)S(1)}, f32[64,4,128]{2,1,0:T(4,128)S(1)}, u32[]{:S(2)}, u32[]{:S(2)}) collective-permute-start(f32[64,4,128]{2,1,0:T(4,128)S(1)} %get-tuple-element.652), channel_id=1, source_target_pairs={{0,4},{4,8},{8,12},{12,16},{16,20},{20,24},{24,28},{28,0},{1,5},{5... | collective-permute-start | bytes 393224 | tf_op jit(solution)/shard_map/while/body/eval_jaxpr/ppermute | solution.py:15
  129.8 8.2 %collective-permute-start.1 = (f32[64,4,128]{2,1,0:T(4,128)S(1)}, f32[64,4,128]{2,1,0:T(4,128)S(1)}, u32[]{:S(2)}, u32[]{:S(2)}) collective-permute-start(f32[64,4,128]{2,1,0:T(4,128)S(1)} %get-tuple-element.652), channel_id=1, source_target_pairs={{0,4},{4,8},{8,12},{12,16},{16,20},{20,24},{24,28},{28,0},{1,5},{5... | collective-permute-start | bytes 393224 | tf_op jit(solution)/shard_map/while/body/eval_jaxpr/ppermute | solution.py:15
  138.4 7.7 %collective-permute-start.1 = (f32[64,4,128]{2,1,0:T(4,128)S(1)}, f32[64,4,128]{2,1,0:T(4,128)S(1)}, u32[]{:S(2)}, u32[]{:S(2)}) collective-permute-start(f32[64,4,128]{2,1,0:T(4,128)S(1)} %get-tuple-element.652), channel_id=1, source_target_pairs={{0,4},{4,8},{8,12},{12,16},{16,20},{20,24},{24,28},{28,0},{1,5},{5... | collective-permute-start | bytes 393224 | tf_op jit(solution)/shard_map/while/body/eval_jaxpr/ppermute | solution.py:15
  146.5 8.4 %collective-permute-start.1 = (f32[64,4,128]{2,1,0:T(4,128)S(1)}, f32[64,4,128]{2,1,0:T(4,128)S(1)}, u32[]{:S(2)}, u32[]{:S(2)}) collective-permute-start(f32[64,4,128]{2,1,0:T(4,128)S(1)} %get-tuple-element.652), channel_id=1, source_target_pairs={{0,4},{4,8},{8,12},{12,16},{16,20},{20,24},{24,28},{28,0},{1,5},{5... | collective-permute-start | bytes 393224 | tf_op jit(solution)/shard_map/while/body/eval_jaxpr/ppermute | solution.py:15
  155.3 9.0 %collective-permute-start.1 = (f32[64,4,128]{2,1,0:T(4,128)S(1)}, f32[64,4,128]{2,1,0:T(4,128)S(1)}, u32[]{:S(2)}, u32[]{:S(2)}) collective-permute-start(f32[64,4,128]{2,1,0:T(4,128)S(1)} %get-tuple-element.652), channel_id=1, source_target_pairs={{0,4},{4,8},{8,12},{12,16},{16,20},{20,24},{24,28},{28,0},{1,5},{5... | collective-permute-start | bytes 393224 | tf_op jit(solution)/shard_map/while/body/eval_jaxpr/ppermute | solution.py:15
  164.7 8.4 %collective-permute-start.1 = (f32[64,4,128]{2,1,0:T(4,128)S(1)}, f32[64,4,128]{2,1,0:T(4,128)S(1)}, u32[]{:S(2)}, u32[]{:S(2)}) collective-permute-start(f32[64,4,128]{2,1,0:T(4,128)S(1)} %get-tuple-element.652), channel_id=1, source_target_pairs={{0,4},{4,8},{8,12},{12,16},{16,20},{20,24},{24,28},{28,0},{1,5},{5... | collective-permute-start | bytes 393224 | tf_op jit(solution)/shard_map/while/body/eval_jaxpr/ppermute | solution.py:15
  173.4 7.8 %collective-permute-start.1 = (f32[64,4,128]{2,1,0:T(4,128)S(1)}, f32[64,4,128]{2,1,0:T(4,128)S(1)}, u32[]{:S(2)}, u32[]{:S(2)}) collective-permute-start(f32[64,4,128]{2,1,0:T(4,128)S(1)} %get-tuple-element.652), channel_id=1, source_target_pairs={{0,4},{4,8},{8,12},{12,16},{16,20},{20,24},{24,28},{28,0},{1,5},{5... | collective-permute-start | bytes 393224 | tf_op jit(solution)/shard_map/while/body/eval_jaxpr/ppermute | solution.py:15
Sparse Core Ops, SparseCore 0:
  92.0 29.6 all-reduce.2
  125.4 73.0 all-reduce.4
